TPU v7x, 128 devices: a whole 4x4x4 slice. The times are simulated.
128 devices in a mesh: tile: 16 (over x, y), view: 8 (over z, core).
Axes of the slice: x: 4, y: 4, z: 4, core: 2. Of those that a mesh axis runs over, the one named last changes fastest.
Arguments:
- estimate: float32 [2, 224, 448, 128], P(None, 'view', 'tile'), may hold values from 0.25 to 4
- view_data: bfloat16 [8, 16, 3, 2, 58, 58, 128], P('view', 'tile'), may hold values from 0.25 to 4
- psf: float32 [6, 3, 31], replicated, may hold values from 0 to 0.5, as said below
- background: float32 [6], replicated, may hold values from 0.1 to 1
- slot_brick: int32 [8, 16, 3], P('view', 'tile'), may hold values from 0 to 15, as said below
- slot_view: int32 [8, 16, 3], P('view', 'tile'), may hold values from 0 to 5, as said below
- intersection: int32 [8, 16, 6], P('view', 'tile'), may hold values from 0 to 1, as said below
Outputs:
- updated: float32 [2, 224, 448, 128], P(None, 'view', 'tile')
Inputs may be any that keep to these rules, and one draw needn't show every extreme that they name: `slot_brick`: within a group, the jobs are exactly the pairs (brick, view) that intersection marks, each once; every brick has at least one view and one brick of each group has all 6; the jobs of a group fill its workers' 3 slots exactly. `slot_view`: the view of each job, consistent with intersection. `intersection`: each brick's row has between 1 and 6 ones. `psf`: all taps are positive.
All inputs are finite; a program needn't handle non-finite values.
Results may differ from a plain program's by a relative error of at most 0.0003.
Values may be sent and summed in bfloat16 or wider, within the bound.
No kernel may reach another device: no remote copies, remote signals or barrier semaphores. Data moves between devices by JAX's collectives and lax.ppermute only.
A program may use at most 128 MiB of HBM per device.

v0:
```python
import jax
import jax.numpy as jnp
from jax import lax
from jax.sharding import PartitionSpec as P


def extended(array, sides, width):
    for axis, dim in sides:
        count, length = (lax.axis_size(axis), array.shape[dim])
        up = [(i, (i + 1) % count) for i in range(count - 1)]
        down = [(j, i) for i, j in up]
        last = lax.slice_in_dim(array, length - width, length, axis=dim)
        leading = lax.slice_in_dim(array, 0, width, axis=dim)
        before = lax.ppermute(last, axis, up)
        after = lax.ppermute(leading, axis, down)
        array = jnp.concatenate([before, array, after], axis=dim)
    return array


def banded(kernel_taps, order, rim_width):
    offsets = jnp.arange(order)[None, :] - jnp.arange(order)[:, None] + rim_width
    matches = offsets[:, :, None] == jnp.arange(kernel_taps.shape[0])[None, None, :]
    return jnp.sum(jnp.where(matches, kernel_taps[None, None, :], 0.0), axis=2)


def forward_blur(block, kernels, rim_width):
    band_x = banded(kernels[0], block.shape[1], rim_width)
    band_y = banded(kernels[1], block.shape[2], rim_width)
    band_z = banded(kernels[2], block.shape[3], rim_width)
    result = jnp.einsum("cxyz,wz->cxyw", block, band_z, precision=lax.Precision.HIGHEST)
    result = jnp.einsum("cxyz,vy->cxvz", result, band_y, precision=lax.Precision.HIGHEST)
    return jnp.einsum("cxyz,ux->cuyz", result, band_x, precision=lax.Precision.HIGHEST)


def backward_blur(ratio, kernels, rim_width, brick_x, brick_y):
    band_x = banded(kernels[0], ratio.shape[1], rim_width)[:, rim_width : rim_width + brick_x]
    band_y = banded(kernels[1], ratio.shape[2], rim_width)[:, rim_width : rim_width + brick_y]
    band_z = banded(kernels[2], ratio.shape[3], rim_width)
    result = jnp.einsum("cxyz,xu->cuyz", ratio, band_x, precision=lax.Precision.HIGHEST)
    result = jnp.einsum("cxyz,yv->cxvz", result, band_y, precision=lax.Precision.HIGHEST)
    return jnp.einsum("cxyz,zw->cxyw", result, band_z, precision=lax.Precision.HIGHEST)


def correction(block, measured, psf, background, view_index, rim_width, brick_x, brick_y):
    kernels = lax.dynamic_index_in_dim(psf, view_index, 0, keepdims=False)
    backdrop = lax.dynamic_index_in_dim(background, view_index, 0, keepdims=False)
    predicted = forward_blur(block, kernels, rim_width) + backdrop
    ratio = measured.astype(jnp.float32) / predicted
    return backward_blur(ratio, kernels, rim_width, brick_x, brick_y)


def on_device(estimate, view_data, psf, background, slot_brick, slot_view, intersection):
    rim_width = psf.shape[2] // 2
    channels, brick_x, brick_y, depth_cells = estimate.shape
    est_wire = estimate.astype(jnp.bfloat16)
    padded = extended(est_wire, (("tile", 2), ("view", 1)), rim_width)
    gathered = lax.all_gather(padded[None], "tile", axis=0, tiled=True)
    owners = lax.axis_size("tile")
    contrib = jnp.zeros((owners, channels, brick_x, brick_y, depth_cells), jnp.float32)
    for slot_index in range(slot_brick.shape[2]):
        brick_index = slot_brick[0, 0, slot_index]
        view_index = slot_view[0, 0, slot_index]
        block = lax.dynamic_index_in_dim(gathered, brick_index, 0, keepdims=False).astype(
            jnp.float32
        )
        factor = correction(
            block,
            view_data[0, 0, slot_index],
            psf,
            background,
            view_index,
            rim_width,
            brick_x,
            brick_y,
        )
        owner_marks = (jnp.arange(owners) == brick_index).astype(jnp.float32)
        contrib = contrib + owner_marks[:, None, None, None, None] * factor[None]
    summed = lax.psum_scatter(contrib, "tile", scatter_dimension=0, tiled=True)[0]
    views_seen = jnp.sum(intersection[0, 0]).astype(jnp.float32)
    return estimate * summed / views_seen


def solution(mesh):
    placed = (
        P(None, "view", "tile", None),
        P("view", "tile", None, None, None, None, None),
        P(),
        P(),
        P("view", "tile", None),
        P("view", "tile", None),
        P("view", "tile", None),
    )
    return jax.shard_map(
        on_device,
        mesh=mesh,
        in_specs=placed,
        out_specs=P(None, "view", "tile", None),
        check_vma=False,
    )
```

profile of v0, /device:TPU:1, one launch (start us, length us, event | category | flops | bytes accessed | tf_op | source)
XLA Modules:
  0.0 482.3 jit_solution(7533203977830049392)
XLA Ops:
  6.5 0.0 all-gather.3.cloned.1.call-start
  6.5 1.2 copy.95
  7.8 0.1 fusion.61
  7.9 4.0 collective-permute-start
  11.9 1.3 collective-permute-start.1
  13.2 2.9 collective-permute-done
  16.2 3.8 collective-permute-done.1
  20.0 0.3 pad_maximum_fusion.1
  20.3 0.0 copy-start.9
  20.3 0.0 copy-start.10
  20.3 0.0 copy-start.11
  20.4 0.0 copy-start.12
  20.4 0.1 fusion.60
  20.5 5.3 %collective-permute-start.2 = (bf16[2,15,58,128]{3,2,1,0:T(8,128)(2,1)S(1)}, bf16[2,15,58,128]{3,2,1,0:T(8,128)(2,1)S(1)}, u32[]{:S(2)}, u32[]{:S(2)}) collective-permute-start(bf16[2,15,58,128]{3,2,1,0:T(8,128)(2,1)S(1)} %get-tuple-element.17), channel_id=1, source_target_pairs={{0,1},{1,2},{2,3},{3,4},{4,5},{5,6},{6,7},{8,9},{9,10},{10,11},{11... | collective-permute-start | bytes 1336328 | tf_op jit(solution)/shard_map/ppermute | solution.py:14
  25.8 1.9 collective-permute-start.3
  27.7 3.8 collective-permute-done.2
  31.5 4.4 collective-permute-done.3
  35.9 1.8 pad_maximum_fusion
  37.7 0.0 all-gather.3.cloned.1.call-update
  37.7 0.0 all-reduce.3.cloned.1.call-start
  37.8 0.0 copy-done.9
  37.8 0.6 fusion.63
  42.0 0.0 copy-done.10
  42.0 0.6 fusion.64
  49.9 0.7 fusion.62
  50.5 1.2 compare_convert_fusion.2
  51.8 1.2 compare_convert_fusion
  53.1 2.0 select_reduce_fusion.7
  55.0 1.2 select_reduce_fusion.2
  56.3 6.5 %fusion.59 = (bf16[1,1,1,2,58,58,128]{6,3,5,4,2,1,0:T(2,128)(2,1)S(1)}, bf16[1,1,1,2,58,58,128]{6,3,5,4,2,1,0:T(2,128)(2,1)S(1)}, bf16[1,1,1,2,58,58,128]{6,3,5,4,2,1,0:T(2,128)(2,1)}) fusion(bf16[1,1,3,2,58,58,128]{6,3,5,4,2,1,0:T(2,128)(2,1)} %param.8), kind=kLoop, calls=%fused_computation.101 | loop fusion | bytes 10334208 | tf_op jit(solution)/shard_map/slice | solution.py:68
  62.8 158.6 %all-gather.3.cloned.1.call-done = bf16[32,58,58,128]{3,2,1,0:T(8,128)(2,1)} async-done(((bf16[2,58,58,128]{3,2,1,0:T(8,128)(2,1)}), bf16[32,58,58,128]{3,2,1,0:T(8,128)(2,1)}) %all-gather.3.cloned.1.call-update) | async-done | bytes 27557904 | tf_op jit(solution)/shard_map/all_gather | solution.py:57
  221.3 3.2 fusion.9
  224.6 3.7 convolution_bitcast_fusion
  228.3 5.5 %fusion = f32[58,2,58,128]{3,0,2,1:T(8,128)S(1)} fusion(f32[2,58,58,128]{3,2,1,0:T(8,128)S(1)} %convolution_bitcast_fusion, f32[58,58]{1,0:T(8,128)S(1)} %copy-done.8), kind=kOutput, calls=%fused_computation.4 | convolution fusion | flops 599384064 | bytes 6902928 | tf_op jit(solution)/shard_map/cxyz,ux->cuyz/dot_general | solution.py:32
  233.7 0.0 copy-start.3
  233.8 3.6 fusion.27
  237.4 2.0 fusion.36
  239.4 0.0 copy-done.3
  239.4 0.9 fusion.41
  240.3 0.6 copy.33
  240.9 3.2 fusion.13
  244.2 3.7 convolution_bitcast_fusion.2
  247.9 0.0 copy-done.7
  247.9 5.9 %fusion.4 = f32[58,2,58,128]{3,0,2,1:T(8,128)S(1)} fusion(f32[2,58,58,128]{3,2,1,0:T(8,128)S(1)} %convolution_bitcast_fusion.2, f32[58,58]{1,0:T(8,128)S(1)} %copy-done.7), kind=kOutput, calls=%fused_computation.8 | convolution fusion | flops 599384064 | bytes 6902928 | tf_op jit(solution)/shard_map/cxyz,ux->cuyz/dot_general | solution.py:32
  253.8 3.4 fusion.29
  257.2 2.0 fusion.30
  259.3 0.0 copy-done.2
  259.3 3.2 fusion.11
  262.5 3.8 convolution_bitcast_fusion.1
  266.4 5.5 %fusion.2 = f32[58,2,58,128]{3,0,2,1:T(8,128)S(1)} fusion(f32[2,58,58,128]{3,2,1,0:T(8,128)S(1)} %convolution_bitcast_fusion.1, f32[58,58]{1,0:T(8,128)S(1)} %copy-done.6), kind=kOutput, calls=%fused_computation.6 | convolution fusion | flops 599384064 | bytes 6902928 | tf_op jit(solution)/shard_map/cxyz,ux->cuyz/dot_general | solution.py:32
  271.9 3.4 fusion.28
  275.3 2.0 fusion.33
  277.3 0.9 fusion.44
  278.2 0.6 copy.27
  278.9 1.1 fusion.47
  280.0 0.6 copy.21
  280.6 10.7 %multiply_add_fusion = f32[16,2,28,28,128]{4,1,3,2,0:T(2,128)} fusion(f32[2,28,28,128]{3,0,2,1:T(2,128)S(1)} %copy.33, f32[2,28,28,128]{3,0,2,1:T(2,128)S(1)} %copy.27, f32[2,28,28,128]{3,0,2,1:T(2,128)S(1)} %copy.21, f32[16]{0:T(128)S(1)} %get-tuple-element.45, f32[16]{0:T(128)S(1)} %get-tuple-element.46, f32[16]{0:T(128)S(1)} %copy-done.13), kind=kLoop, calls=%fused_computation | loop fusion | flops 16056320 | bytes 15253696 | tf_op jit(solution)/shard_map/add | solution.py:77
  291.3 0.0 all-reduce.3.cloned.1.call-update
  291.3 0.6 copy-done.14
  292.0 0.6 reduce_sum.104
  293.3 0.0 copy-done.15
  293.3 0.6 dynamic-slice
  293.9 178.2 %all-reduce.3.cloned.1.call-done = f32[16,2,28,28,128]{4,1,3,2,0:T(2,128)} async-done(((f32[16,2,28,28,128]{4,1,3,2,0:T(2,128)}), f32[16,2,28,28,128]{4,1,3,2,0:T(2,128)}) %all-reduce.3.cloned.1.call-update) | async-done | bytes 12845072
  472.1 3.1 fusion.40
  (25 shorter events, 0.1 us)
Async XLA Ops:
  6.5 214.8 %all-gather.3.cloned.1.call-start = ((), (), s32[]{:S(2)}) async-start(), calls=%async_computation | async-start | bytes 32309248 | tf_op jit(solution)/shard_map/all_gather | solution.py:57
  7.9 8.3 %collective-permute-start = (bf16[2,28,15,128]{3,2,1,0:T(8,128)(2,1)S(1)}, bf16[2,28,15,128]{3,2,1,0:T(8,128)(2,1)S(1)}, u32[]{:S(2)}, u32[]{:S(2)}) collective-permute-start(bf16[2,28,15,128]{3,2,1,0:T(8,128)(2,1)S(1)} %get-tuple-element.19), channel_id=1, source_target_pairs={{0,8},{8,16},{16,24},{24,32},{32,40},{40,48},{48,56},{56,64},{64,7... | collective-permute-start | bytes 645128 | tf_op jit(solution)/shard_map/ppermute | solution.py:14
  11.9 8.0 %collective-permute-start.1 = (bf16[2,28,15,128]{3,2,1,0:T(8,128)(2,1)S(1)}, bf16[2,28,15,128]{3,2,1,0:T(8,128)(2,1)S(1)}, u32[]{:S(2)}, u32[]{:S(2)}) collective-permute-start(bf16[2,28,15,128]{3,2,1,0:T(8,128)(2,1)S(1)} %get-tuple-element.20), channel_id=1, source_target_pairs={{8,0},{16,8},{24,16},{32,24},{40,32},{48,40},{56,48},{64,56},{72,6... | collective-permute-start | bytes 645128 | tf_op jit(solution)/shard_map/ppermute | solution.py:15
  20.3 17.4 %copy-start.9 = (s32[1,1,3]{2,1,0:T(1,128)S(1)}, s32[1,1,3]{2,1,0:T(1,128)}, u32[]{:S(2)}) copy-start(s32[1,1,3]{2,1,0:T(1,128)} %param.11) | copy-start | bytes 40
  20.3 21.7 %copy-start.10 = (s32[1,1,3]{2,1,0:T(1,128)S(1)}, s32[1,1,3]{2,1,0:T(1,128)}, u32[]{:S(2)}) copy-start(s32[1,1,3]{2,1,0:T(1,128)} %param.12) | copy-start | bytes 40
  20.3 29.5 %copy-start.11 = (f32[6]{0:T(128)S(1)}, f32[6]{0:T(128)}, u32[]{:S(2)}) copy-start(f32[6]{0:T(128)} %param.10) | copy-start | bytes 76
  20.4 32.6 %copy-start.12 = (f32[6,3,31]{2,1,0:T(4,128)S(1)}, f32[6,3,31]{2,1,0:T(4,128)}, u32[]{:S(2)}) copy-start(f32[6,3,31]{2,1,0:T(4,128)} %param.9) | copy-start | bytes 6700
  20.5 11.1 %collective-permute-start.2 = (bf16[2,15,58,128]{3,2,1,0:T(8,128)(2,1)S(1)}, bf16[2,15,58,128]{3,2,1,0:T(8,128)(2,1)S(1)}, u32[]{:S(2)}, u32[]{:S(2)}) collective-permute-start(bf16[2,15,58,128]{3,2,1,0:T(8,128)(2,1)S(1)} %get-tuple-element.17), channel_id=1, source_target_pairs={{0,1},{1,2},{2,3},{3,4},{4,5},{5,6},{6,7},{8,9},{9,10},{10,11},{11... | collective-permute-start | bytes 1336328 | tf_op jit(solution)/shard_map/ppermute | solution.py:14
  25.8 10.1 %collective-permute-start.3 = (bf16[2,15,58,128]{3,2,1,0:T(8,128)(2,1)S(1)}, bf16[2,15,58,128]{3,2,1,0:T(8,128)(2,1)S(1)}, u32[]{:S(2)}, u32[]{:S(2)}) collective-permute-start(bf16[2,15,58,128]{3,2,1,0:T(8,128)(2,1)S(1)} %get-tuple-element.18), channel_id=1, source_target_pairs={{1,0},{2,1},{3,2},{4,3},{5,4},{6,5},{7,6},{9,8},{10,9},{11,10},{12... | collective-permute-start | bytes 1336328 | tf_op jit(solution)/shard_map/ppermute | solution.py:15
  37.7 434.4 %all-reduce.3.cloned.1.call-start = ((), (), s32[]{:S(2)}) async-start(), calls=%async_computation.1 | async-start | bytes 25690112
  221.3 3.3 copy-start.5
  224.6 3.7 copy-start.8
  228.3 5.5 %copy-start.1 = (bf16[1,1,1,2,58,58,128]{6,3,5,4,2,1,0:T(2,128)(2,1)S(1)}, bf16[1,1,1,2,58,58,128]{6,3,5,4,2,1,0:T(2,128)(2,1)}, u32[]{:S(2)}) copy-start(bf16[1,1,1,2,58,58,128]{6,3,5,4,2,1,0:T(2,128)(2,1)} %get-tuple-element.16) | copy-start | bytes 5167108
  233.7 5.7 %copy-start.3 = (f32[128,128]{1,0:T(8,128)S(1)}, f32[128,128]{1,0:T(8,128)}, u32[]{:S(2)}) copy-start(f32[128,128]{1,0:T(8,128)} %get-tuple-element.6) | copy-start | bytes 196612
  240.3 3.9 copy-start.4
  244.2 3.7 copy-start.7
  253.8 5.5 %copy-start.2 = (f32[128,128]{1,0:T(8,128)S(1)}, f32[128,128]{1,0:T(8,128)}, u32[]{:S(2)}) copy-start(f32[128,128]{1,0:T(8,128)} %get-tuple-element.7) | copy-start | bytes 196612
  262.5 3.9 copy-start.6
  277.3 3.3 copy-start.13
  291.3 0.7 copy-start.14
  291.3 1.9 copy-start.15
  291.3 180.8 %copy-start = (f32[2,28,28,128]{3,0,2,1:T(2,128)S(1)}, f32[2,28,28,128]{3,0,2,1:T(2,128)}, u32[]{:S(2)}) copy-start(f32[2,28,28,128]{3,0,2,1:T(2,128)} %param.7) | copy-start | bytes 2408452
Sparse Core Ops, SparseCore 0:
  37.8 183.4 all-gather.2
  291.5 180.6 all-reduce.2
where the time goes:
time: 487 us; the launch traced here: 482 us
  waiting for transfers between devices  352 us (72%)
  matrix products  57.1 us (12%)
  between operations  25.6 us (5%)
  other arithmetic  22.1 us (5%)
  local copies, waits for them, and re-layouts  13 us (3%)
  starting transfers between devices  12.6 us (3%)
    unnamed x3, waiting for transfers between devices  178 us
    all_gather x1, waiting for transfers between devices, on_device(): gathered = lax.all_gather(padded[None], 'tile', axis=0, tiled=True)  159 us
    dot_general x3, matrix products, forward_blur(): jnp.einsum('cxyz,ux->cuyz', result, band_x, precision=lax.Precision.HIGHEST)  16.8 us
    dot_general x3, matrix products, forward_blur(): jnp.einsum('cxyz,vy->cxvz', result, band_y, precision=lax.Precision.HIGHEST)  11.1 us
    add x1, other arithmetic, on_device(): contrib = contrib + owner_marks[:, None, None, None, None] * factor[None]  10.7 us
    dot_general x3, matrix products, backward_blur(): jnp.einsum('cxyz,xu->cuyz', ratio, band_x, precision=lax.Precision.HIGHEST)  10.5 us
  transfers between devices with their start and end apart: 6, of which 6 were waited for; matrix products, arithmetic and copies ran while one was open for 3% of the time, Pallas kernels for 0%

commit v1 on v0

--- a/solution.py
+++ b/solution.py
@@ -54,7 +54,9 @@
     channels, brick_x, brick_y, depth_cells = estimate.shape
     est_wire = estimate.astype(jnp.bfloat16)
     padded = extended(est_wire, (("tile", 2), ("view", 1)), rim_width)
-    gathered = lax.all_gather(padded[None], "tile", axis=0, tiled=True)
+    gathered = jnp.concatenate(
+        lax.all_to_all(jnp.stack([padded[None]] * lax.axis_size("tile")), "tile", 0, 0), axis=0
+    )
     owners = lax.axis_size("tile")
     contrib = jnp.zeros((owners, channels, brick_x, brick_y, depth_cells), jnp.float32)
     for slot_index in range(slot_brick.shape[2]):

time: 487 us -> 874 us (1.79)
  waiting for transfers between devices: 352 us -> 686 us
  other arithmetic: 22.1 us -> 44.8 us
  local copies, waits for them, and re-layouts: 13 us -> 35.3 us
  starting transfers between devices: 12.6 us -> 23.8 us
    all_to_all x0 -> x1, waiting for transfers between devices: none -> 467 us  [on_device(): lax.all_to_all(jnp.stack([padded[None]] * lax.axis_size('tile')), 'tile',...]
    all_gather x1 -> x0, waiting for transfers between devices: 159 us -> none  [on_device(): gathered = lax.all_gather(padded[None], 'tile', axis=0, tiled=True)]
    unnamed x3 -> x2, waiting for transfers between devices: 178 us -> 211 us
    concatenate x2, other arithmetic: 2.09 us -> 23.3 us  [extended(): array = jnp.concatenate([before, array, after], axis=dim)]
    another operation x0 -> x1, local copies, waits for them, and re-layouts: none -> 16.5 us  [on_device(): jnp.stack([padded[None]] * lax.axis_size('tile'))]
    all_to_all x0 -> x1, starting transfers between devices: none -> 9.89 us  [on_device(): lax.all_to_all(jnp.stack([padded[None]] * lax.axis_size('tile')), 'tile',...]
  transfers between devices with their start and end apart: 6 -> 6, of which waited for: 6 -> 6; matrix products, arithmetic and copies ran while one was open for 3% -> 2% of each run, Pallas kernels for 0% -> 0%
where the time goes in v1:
time: 874 us; the launch traced here: 867 us
  waiting for transfers between devices  686 us (78%)
  matrix products  50.8 us (6%)
  other arithmetic  44.8 us (5%)
  local copies, waits for them, and re-layouts  35.3 us (4%)
  between operations  26.1 us (3%)
  starting transfers between devices  23.8 us (3%)
    all_to_all x1, waiting for transfers between devices, on_device(): lax.all_to_all(jnp.stack([padded[None]] * lax.axis_size('tile')), 'tile',...  467 us
    unnamed x2, waiting for transfers between devices  211 us
    concatenate x2, other arithmetic, extended(): array = jnp.concatenate([before, array, after], axis=dim)  23.3 us
  transfers between devices with their start and end apart: 6, of which 6 were waited for; matrix products, arithmetic and copies ran while one was open for 2% of the time, Pallas kernels for 0%

profile of v1, /device:TPU:1, one launch (start us, length us, event | category | flops | bytes accessed | tf_op | source)
XLA Modules:
  0.0 867.1 jit_solution(2384236197969427295)
XLA Ops:
  6.5 1.4 convert_element_type.51
  8.0 0.3 fusion.58
  8.3 1.3 collective-permute-start.1
  9.6 4.7 collective-permute-start
  14.2 2.7 collective-permute-done.1
  16.9 0.9 collective-permute-done
  17.8 1.2 pad_maximum_fusion.1
  19.0 0.6 fusion.57
  19.6 3.9 collective-permute-start.3
  23.4 3.6 collective-permute-start.2
  27.0 4.1 collective-permute-done.3
  31.1 1.2 collective-permute-done.2
  32.3 22.1 %pad_maximum_fusion = bf16[2,58,58,128]{3,0,2,1:T(2,128)(2,1)S(1)} fusion(bf16[2,15,58,128]{3,0,2,1:T(2,128)(2,1)S(1)} %collective-permute-done.3, bf16[2,28,15,128]{3,0,2,1:T(2,128)(2,1)S(1)} %collective-permute-done.1, bf16[2,28,28,128]{3,0,2,1:T(2,128)(2,1)S(1)} %convert_element_type.51, bf16[2,28,15,128]{3,0,2,1:T(2,128)(2,1)S(1)} %collective-permute-done, ...), kind=kLoop, calls=%fused_computation.41 | loop fusion | flops 3444736 | bytes 3444736 | tf_op jit(solution)/shard_map/concatenate | solution.py:16
  54.4 16.5 %stack.3 = bf16[16,1,2,58,58,128]{5,2,4,3,1,0:T(2,128)(2,1)} broadcast(bf16[2,58,58,128]{3,0,2,1:T(2,128)(2,1)S(1)} %pad_maximum_fusion), dimensions={2,3,4,5} | broadcast | bytes 29280256 | tf_op jit(solution)/shard_map/stack | solution.py:58
  70.9 0.0 copy-start.12
  70.9 9.9 %all-to-all-start = ((bf16[16,1,2,58,58,128]{5,2,4,3,1,0:T(2,128)(2,1)}), bf16[16,1,2,58,58,128]{5,2,4,3,1,0:T(2,128)(2,1)}, u32[]{:S(2)}, u32[]{:S(2)}) async-start(bf16[16,1,2,58,58,128]{5,2,4,3,1,0:T(2,128)(2,1)} %stack.3), calls=%async_computation | async-start | bytes 55115776 | tf_op jit(solution)/shard_map/all_to_all | solution.py:58
  80.8 0.5 all-reduce.3.cloned.1.call-start
  81.3 0.0 copy-done.9
  81.4 0.6 fusion.60
  85.9 0.6 fusion.61
  94.0 0.7 fusion.59
  94.7 1.2 compare_convert_fusion.2
  95.9 1.3 compare_convert_fusion
  97.2 0.0 copy-done.12
  97.3 1.9 select_reduce_fusion.7
  99.2 1.2 select_reduce_fusion.2
  100.4 6.3 fusion.56
  106.7 466.9 %all-to-all-done = bf16[16,1,2,58,58,128]{5,2,4,3,1,0:T(2,128)(2,1)} async-done(((bf16[16,1,2,58,58,128]{5,2,4,3,1,0:T(2,128)(2,1)}), bf16[16,1,2,58,58,128]{5,2,4,3,1,0:T(2,128)(2,1)}, u32[]{:S(2)}, u32[]{:S(2)}) %all-to-all-start) | async-done | bytes 27557920 | tf_op jit(solution)/shard_map/all_to_all | solution.py:58
  573.7 6.1 constant_dynamic-slice_fusion.4
  579.8 1.7 fusion.9
  581.5 0.0 copy-done.5
  581.5 0.0 copy-start.8
  581.5 3.6 convolution_bitcast_fusion
  585.1 0.0 copy-done.8
  585.1 0.0 copy-start.1
  585.2 5.6 fusion
  590.8 0.0 copy-done.1
  590.8 3.3 fusion.27
  594.1 2.0 fusion.36
  596.1 0.9 fusion.41
  597.0 0.6 copy.35
  597.6 1.7 fusion.11
  599.4 3.8 convolution_bitcast_fusion.1
  603.2 0.0 copy-done.7
  603.2 5.2 fusion.2
  608.5 3.2 fusion.28
  611.7 2.0 fusion.33
  613.8 0.9 fusion.44
  614.6 1.0 copy.28
  615.7 1.7 fusion.13
  617.4 3.4 convolution_bitcast_fusion.2
  620.8 5.2 fusion.4
  626.0 3.6 fusion.29
  629.6 2.0 fusion.30
  631.7 0.9 fusion.47
  632.5 0.6 copy.21
  633.2 0.0 copy-done.13
  633.2 10.7 %multiply_add_fusion = f32[16,2,28,28,128]{4,1,3,2,0:T(2,128)} fusion(f32[2,28,28,128]{3,0,2,1:T(2,128)S(1)} %copy.35, f32[2,28,28,128]{3,0,2,1:T(2,128)S(1)} %copy.28, f32[2,28,28,128]{3,0,2,1:T(2,128)S(1)} %copy.21, f32[16]{0:T(128)S(1)} %get-tuple-element.48, f32[16]{0:T(128)S(1)} %get-tuple-element.49, f32[16]{0:T(128)S(1)} %copy-done.13), kind=kLoop, calls=%fused_computation | loop fusion | flops 16056320 | bytes 15253696 | tf_op jit(solution)/shard_map/add | solution.py:79
  643.9 0.0 all-reduce.3.cloned.1.call-update
  643.9 0.6 copy-done.14
  644.5 0.6 reduce_sum.104
  645.8 0.6 dynamic-slice.3
  646.4 210.6 %all-reduce.3.cloned.1.call-done = f32[16,2,28,28,128]{4,1,3,2,0:T(2,128)} async-done(((f32[16,2,28,28,128]{4,1,3,2,0:T(2,128)}), f32[16,2,28,28,128]{4,1,3,2,0:T(2,128)}) %all-reduce.3.cloned.1.call-update) | async-done | bytes 12845072
  857.0 3.1 fusion.40
  (26 shorter events, 0.1 us)
Async XLA Ops:
  8.3 8.6 collective-permute-start.1
  9.6 8.2 collective-permute-start
  19.6 11.6 %collective-permute-start.3 = (bf16[2,15,58,128]{3,0,2,1:T(2,128)(2,1)S(1)}, bf16[2,15,58,128]{3,0,2,1:T(2,128)(2,1)S(1)}, u32[]{:S(2)}, u32[]{:S(2)}) collective-permute-start(bf16[2,15,58,128]{3,0,2,1:T(2,128)(2,1)S(1)} %get-tuple-element.21), channel_id=1, source_target_pairs={{1,0},{2,1},{3,2},{4,3},{5,4},{6,5},{7,6},{9,8},{10,9},{11,10},{12... | collective-permute-start | bytes 1336328 | tf_op jit(solution)/shard_map/ppermute | solution.py:15
  23.4 8.9 %collective-permute-start.2 = (bf16[2,15,58,128]{3,0,2,1:T(2,128)(2,1)S(1)}, bf16[2,15,58,128]{3,0,2,1:T(2,128)(2,1)S(1)}, u32[]{:S(2)}, u32[]{:S(2)}) collective-permute-start(bf16[2,15,58,128]{3,0,2,1:T(2,128)(2,1)S(1)} %get-tuple-element.20), channel_id=1, source_target_pairs={{0,1},{1,2},{2,3},{3,4},{4,5},{5,6},{6,7},{8,9},{9,10},{10,11},{11... | collective-permute-start | bytes 1336328 | tf_op jit(solution)/shard_map/ppermute | solution.py:14
  70.9 10.4 %copy-start.9 = (s32[1,1,3]{2,1,0:T(1,128)S(1)}, s32[1,1,3]{2,1,0:T(1,128)}, u32[]{:S(2)}) copy-start(s32[1,1,3]{2,1,0:T(1,128)} %param.11) | copy-start | bytes 40
  70.9 15.0 %copy-start.10 = (s32[1,1,3]{2,1,0:T(1,128)S(1)}, s32[1,1,3]{2,1,0:T(1,128)}, u32[]{:S(2)}) copy-start(s32[1,1,3]{2,1,0:T(1,128)} %param.12) | copy-start | bytes 40
  70.9 23.1 %copy-start.11 = (f32[6]{0:T(128)S(1)}, f32[6]{0:T(128)}, u32[]{:S(2)}) copy-start(f32[6]{0:T(128)} %param.10) | copy-start | bytes 76
  70.9 26.3 %copy-start.12 = (f32[6,3,31]{2,1,0:T(4,128)S(1)}, f32[6,3,31]{2,1,0:T(4,128)}, u32[]{:S(2)}) copy-start(f32[6,3,31]{2,1,0:T(4,128)} %param.9) | copy-start | bytes 6700
  70.9 502.7 %all-to-all-start = ((bf16[16,1,2,58,58,128]{5,2,4,3,1,0:T(2,128)(2,1)}), bf16[16,1,2,58,58,128]{5,2,4,3,1,0:T(2,128)(2,1)}, u32[]{:S(2)}, u32[]{:S(2)}) async-start(bf16[16,1,2,58,58,128]{5,2,4,3,1,0:T(2,128)(2,1)} %stack.3), calls=%async_computation | async-start | bytes 55115776 | tf_op jit(solution)/shard_map/all_to_all | solution.py:58
  80.8 776.2 %all-reduce.3.cloned.1.call-start = ((), (), s32[]{:S(2)}) async-start(), calls=%async_computation.1 | async-start | bytes 25690112
  573.7 6.1 copy-start.3
  579.7 1.8 copy-start.5
  581.5 3.6 copy-start.8
  585.1 5.6 copy-start.1
  594.1 3.6 copy-start.2
  597.0 2.4 copy-start.4
  599.4 3.9 copy-start.7
  617.3 3.4 copy-start.6
  629.6 3.6 copy-start.13
  643.9 0.7 copy-start.14
  643.9 1.9 copy-start.15
  643.9 213.1 %copy-start = (f32[2,28,28,128]{3,0,2,1:T(2,128)S(1)}, f32[2,28,28,128]{3,0,2,1:T(2,128)}, u32[]{:S(2)}) copy-start(f32[2,28,28,128]{3,0,2,1:T(2,128)} %param.7) | copy-start | bytes 2408452
Sparse Core Ops, SparseCore 0:
  644.0 212.9 all-reduce.2
